TPU v7x, 32 devices: a whole 2x2x4 slice. The times are simulated.
32 devices in a mesh: rep: 8 (over y, x, core), fsdp: 4 (over z).
Axes of the slice: x: 2, y: 2, z: 4, core: 2. Of those that a mesh axis runs over, the one named last changes fastest.
Arguments:
- base: float32 [3, 32, 8192], P(None, 'fsdp'), may hold values from -6 to 6
- local: float32 [8, 3, 32, 8192], P('rep', None, 'fsdp'), may hold values from -6 to 6
- momentum: float32 [3, 32, 8192], P(None, 'fsdp', 'rep'), may hold values from -3 to 3
- hidden: bfloat16 [8, 512, 32], P('rep', 'fsdp'), may hold values from -6 to 6
- out_grad: bfloat16 [8, 512, 8192], P('rep', 'fsdp'), may hold values from -0.06591797 to 0.06591797
Outputs:
- mixed: float32 [8, 3, 32, 8192], P('rep', None, 'fsdp')
- momentum_out: float32 [3, 32, 8192], P(None, 'fsdp', 'rep')
- input_grad: bfloat16 [8, 512, 32], P('rep', 'fsdp')
- weight_grad: float32 [8, 32, 8192], P('rep', 'fsdp')
All inputs are finite; a program needn't handle non-finite values.
Results may differ from a plain program's by a relative error of at most 0.015.
Values may be sent and summed in bfloat16 or wider, within the bound.
No kernel may reach another device: no remote copies, remote signals or barrier semaphores. Data moves between devices by JAX's collectives and lax.ppermute only.
A program may use at most 64 MiB of HBM per device.

v0:
```python
import jax
import jax.numpy as jnp
from jax import lax
from jax.sharding import PartitionSpec as P

outer_beta = 0.9
outer_rate = 0.7
mix_keep = 0.5


def per_device(base, local, momentum, hidden, out_grad):
    replica_count = lax.axis_size("rep")
    weights = local[0, 2].astype(jnp.bfloat16)
    grads_here = out_grad[0]
    activations = hidden[0]
    input_grad = lax.dot_general(
        grads_here,
        lax.all_gather(weights, "fsdp", axis=0, tiled=True),
        (((1,), (1,)), ((), ())),
        preferred_element_type=jnp.float32,
    ).astype(jnp.bfloat16)
    weight_grad = lax.psum_scatter(
        lax.dot_general(
            activations, grads_here, (((0,), (0,)), ((), ())), preferred_element_type=jnp.float32
        ).astype(jnp.bfloat16),
        "fsdp",
        scatter_dimension=0,
        tiled=True,
    ).astype(jnp.float32)
    drift = base - local[0]
    share_width = momentum.shape[2]
    share_start = lax.axis_index("rep") * share_width
    delta = lax.psum(drift, "rep") / replica_count
    moment_all = lax.all_gather(momentum, "rep", axis=2, tiled=True)
    moment_new = outer_beta * moment_all + delta
    updated = base - outer_rate * (delta + outer_beta * moment_new)
    momentum_out = lax.dynamic_slice_in_dim(moment_new, share_start, share_width, 2)
    mixed = mix_keep * local[0] + (1.0 - mix_keep) * updated
    return (mixed[None], momentum_out, input_grad[None], weight_grad[None])


def solution(mesh):
    return jax.shard_map(
        per_device,
        mesh=mesh,
        in_specs=(
            P(None, "fsdp", None),
            P("rep", None, "fsdp", None),
            P(None, "fsdp", "rep"),
            P("rep", "fsdp", None),
            P("rep", "fsdp", None),
        ),
        out_specs=(
            P("rep", None, "fsdp", None),
            P(None, "fsdp", "rep"),
            P("rep", "fsdp", None),
            P("rep", "fsdp", None),
        ),
        check_vma=False,
    )
```

profile of v0, /device:TPU:0, one launch (start us, length us, event | category | flops | bytes accessed | tf_op | source)
XLA Modules:
  0.0 83.5 jit_solution(2399152442900048808)
XLA Ops:
  8.0 0.0 copy-start
  8.0 0.0 copy-start.3
  8.0 0.0 all-reduce.2.cloned.1.call-start
  8.1 2.5 %bitcast_subtract_fusion = f32[3,8,8192]{2,1,0:T(8,128)} fusion(f32[3,8,8192]{2,1,0:T(8,128)} %param.5, f32[1,3,8,8192]{3,2,1,0:T(8,128)} %param.6), kind=kLoop, calls=%fused_computation.7 | loop fusion | flops 196608 | bytes 2359296 | tf_op jit(solution)/shard_map/sub | solution.py:30
  10.5 0.0 copy-start.1
  10.5 0.0 copy-start.2
  10.5 0.0 all-reduce.2.cloned.1.call-update
  10.6 0.0 reduce-scatter.2.cloned.1.call-start
  10.6 0.0 copy-done
  10.6 0.0 copy-done.3
  10.6 1.2 %convolution_convert_fusion = bf16[32,8192]{1,0:T(8,128)(2,1)} fusion(bf16[1,128,8192]{2,1,0:T(8,128)(2,1)S(1)} %copy-done, bf16[1,128,32]{1,2,0:T(8,128)(2,1)S(1)} %copy-done.3), kind=kOutput, calls=%fused_computation | convolution fusion | flops 67371008 | bytes 2629632 | tf_op jit(solution)/shard_map/dot_general | solution.py:23
  11.8 0.0 reduce-scatter.2.cloned.1.call-update
  11.9 0.0 copy-done.1
  11.9 0.0 copy-done.2
  11.9 14.0 %all_gather.6 = f32[3,8,8192]{2,1,0:T(8,128)} all-gather(f32[3,8,1024]{2,1,0:T(8,128)S(1)} %copy-done.2), channel_id=1, replica_groups=mesh['rep'=8,'fsdp'=4] {'rep'}, dimensions={2}, use_global_device_ids=true | all-gather | bytes 884736 | tf_op jit(solution)/shard_map/all_gather | solution.py:34
  25.9 18.9 %all-gather = bf16[1,1,32,8192]{3,2,1,0:T(8,128)(2,1)S(1)} all-gather(bf16[1,1,8,8192]{3,2,1,0:T(8,128)(2,1)S(1)} %slice.7), channel_id=2, replica_groups=mesh['rep'=8,'fsdp'=4] {'fsdp'}, dimensions={2}, use_global_device_ids=true | all-gather | bytes 655360 | tf_op jit(solution)/shard_map/all_gather | solution.py:18
  44.8 1.4 %fusion.6 = bf16[1,128,32]{1,2,0:T(8,128)(2,1)} fusion(bf16[1,128,8192]{2,1,0:T(8,128)(2,1)S(1)} %copy-done, bf16[1,1,32,8192]{3,2,1,0:T(8,128)(2,1)S(1)} %all-gather), kind=kOutput, calls=%fused_computation.5 | convolution fusion | flops 67112960 | bytes 2629632 | tf_op jit(solution)/shard_map/dot_general | solution.py:16
  46.2 24.9 %all-reduce.2.cloned.1.call-done = f32[3,8,8192]{2,1,0:T(8,128)} async-done(((f32[3,8,8192]{2,1,0:T(8,128)}), f32[3,8,8192]{2,1,0:T(8,128)}) %all-reduce.2.cloned.1.call-update) | async-done | bytes 786448 | tf_op jit(solution)/shard_map/psum | solution.py:33
  71.1 2.7 %multiply_add_fusion = (f32[3,8,8192]{2,1,0:T(8,128)S(1)}, f32[1,3,8,8192]{3,2,1,0:T(8,128)}) fusion(f32[3,8,8192]{2,1,0:T(8,128)} %all_gather.6, f32[3,8,8192]{2,1,0:T(8,128)} %all-reduce.2.cloned.1.call-done, f32[3,8,8192]{2,1,0:T(8,128)} %param.5, f32[1,3,8,8192]{3,2,1,0:T(8,128)S(1)} %copy-done.1), kind=kLoop, calls=%fused_computation.10 | loop fusion | flops 1769472 | bytes 4718592 | tf_op jit(solution)/shard_map/add | solution.py:35
  73.8 0.6 constant_dynamic-slice_fusion
  74.5 0.0 reduce-scatter.2.cloned.1.call-done
  74.5 1.6 %bitcast_convert_fusion = f32[1,8,8192]{2,1,0:T(8,128)} fusion(bf16[8,8192]{1,0:T(8,128)(2,1)} %reduce-scatter.2.cloned.1.call-done), kind=kLoop, calls=%fused_computation.13 | loop fusion | flops 65536 | bytes 393216 | tf_op jit(solution)/shard_map/broadcast_in_dim | solution.py:39
  (1 shorter events, 0.0 us)
Async XLA Ops:
  8.0 2.6 %copy-start = (bf16[1,128,8192]{2,1,0:T(8,128)(2,1)S(1)}, bf16[1,128,8192]{2,1,0:T(8,128)(2,1)}, u32[]{:S(2)}) copy-start(bf16[1,128,8192]{2,1,0:T(8,128)(2,1)} %param.9) | copy-start | bytes 6291460
  8.0 2.6 %copy-start.3 = (bf16[1,128,32]{1,2,0:T(8,128)(2,1)S(1)}, bf16[1,128,32]{1,2,0:T(8,128)(2,1)}, u32[]{:S(2)}) copy-start(bf16[1,128,32]{1,2,0:T(8,128)(2,1)} %param.8) | copy-start | bytes 24580
  8.0 63.1 %all-reduce.2.cloned.1.call-start = ((), (), s32[]{:S(2)}) async-start(), calls=%async_computation.1 | async-start | bytes 1572864 | tf_op jit(solution)/shard_map/psum | solution.py:33
  10.5 1.3 %copy-start.1 = (f32[1,3,8,8192]{3,2,1,0:T(8,128)S(1)}, f32[1,3,8,8192]{3,2,1,0:T(8,128)}, u32[]{:S(2)}) copy-start(f32[1,3,8,8192]{3,2,1,0:T(8,128)} %param.6) | copy-start | bytes 2359300
  10.5 1.4 %copy-start.2 = (f32[3,8,1024]{2,1,0:T(8,128)S(1)}, f32[3,8,1024]{2,1,0:T(8,128)}, u32[]{:S(2)}) copy-start(f32[3,8,1024]{2,1,0:T(8,128)} %param.7) | copy-start | bytes 294916
  10.6 63.9 %reduce-scatter.2.cloned.1.call-start = ((), (), s32[]{:S(2)}) async-start(), calls=%async_computation.2 | async-start | bytes 655360 | tf_op jit(solution)/shard_map/reduce_scatter | solution.py:22
Sparse Core Ops, SparseCore 0:
  12.5 58.4 all-reduce.1
Sparse Core Ops, SparseCore 1:
  13.3 24.8 reduce-scatter.1
where the time goes:
time: 83.7 us; the launch traced here: 83.5 us
  blocking collectives  32.9 us (39%)
  waiting for transfers between devices  24.9 us (30%)
  between operations  15.5 us (19%)
  other arithmetic  6.82 us (8%)
  matrix products  2.62 us (3%)
    psum x1, waiting for transfers between devices, per_device(): delta = lax.psum(drift, 'rep') / replica_count  24.9 us
    all_gather x1, blocking collectives, per_device(): lax.all_gather(weights, 'fsdp', axis=0, tiled=True)  18.9 us
    all_gather x1, blocking collectives, per_device(): moment_all = lax.all_gather(momentum, 'rep', axis=2, tiled=True)  14 us
    add x1, other arithmetic, per_device(): moment_new = outer_beta * moment_all + delta  2.73 us
    sub x1, other arithmetic, per_device(): drift = base - local[0]  2.47 us
  transfers between devices with their start and end apart: 2, of which 1 were waited for; matrix products, arithmetic and copies ran while one was open for 7% of the time, Pallas kernels for 0%

commit v1 on v0

--- a/solution.py
+++ b/solution.py
@@ -6,6 +6,12 @@
 outer_beta = 0.9
 outer_rate = 0.7
 mix_keep = 0.5
+
+
+def add_all(x, axis):
+    parts = lax.all_gather(x, axis, axis=0, tiled=False)
+    total = parts.sum(axis=0)
+    return total
 
 
 def per_device(base, local, momentum, hidden, out_grad):
@@ -30,7 +36,7 @@
     drift = base - local[0]
     share_width = momentum.shape[2]
     share_start = lax.axis_index("rep") * share_width
-    delta = lax.psum(drift, "rep") / replica_count
+    delta = add_all(drift, "rep") / replica_count
     moment_all = lax.all_gather(momentum, "rep", axis=2, tiled=True)
     moment_new = outer_beta * moment_all + delta
     updated = base - outer_rate * (delta + outer_beta * moment_new)

time: 83.7 us -> 77.7 us (0.928)
  waiting for transfers between devices: 24.9 us -> 14.7 us
  other arithmetic: 6.82 us -> 10.5 us
  blocking collectives: 32.9 us -> 31 us
  local copies, waits for them, and re-layouts: 0.68 us -> 2.2 us
    psum x1 -> x0, waiting for transfers between devices: 24.9 us -> none  [per_device(): delta = lax.psum(drift, 'rep') / replica_count]
    all_gather x0 -> x1, waiting for transfers between devices: none -> 14.7 us  [add_all(): parts = lax.all_gather(x, axis, axis=0, tiled=False)]
    reduce_sum x0 -> x1, other arithmetic: none -> 4.05 us  [add_all(): total = parts.sum(axis=0)]
    unnamed x8 -> x6, local copies, waits for them, and re-layouts: 0.02 us -> 1.54 us
    all_gather x1, blocking collectives: 14 us -> 12.9 us  [per_device(): moment_all = lax.all_gather(momentum, 'rep', axis=2, tiled=True)]
where the time goes in v1:
time: 77.7 us; the launch traced here: 77.4 us
  blocking collectives  31 us (40%)
  between operations  15.5 us (20%)
  waiting for transfers between devices  14.7 us (19%)
  other arithmetic  10.5 us (14%)
  matrix products  3.33 us (4%)
  local copies, waits for them, and re-layouts  2.2 us (3%)
    all_gather x1, blocking collectives, per_device(): lax.all_gather(weights, 'fsdp', axis=0, tiled=True)  18.1 us
    all_gather x1, waiting for transfers between devices, add_all(): parts = lax.all_gather(x, axis, axis=0, tiled=False)  14.7 us
    all_gather x1, blocking collectives, per_device(): moment_all = lax.all_gather(momentum, 'rep', axis=2, tiled=True)  12.9 us
    reduce_sum x1, other arithmetic, add_all(): total = parts.sum(axis=0)  4.05 us
    add x1, other arithmetic, per_device(): moment_new = outer_beta * moment_all + delta  2.73 us
    sub x1, other arithmetic, per_device(): drift = base - local[0]  2.1 us
    dot_general x1, matrix products, per_device(): lax.dot_general(activations, grads_here, (((0,), (0,)), ((), ())), prefer...  1.91 us
    broadcast_in_dim x1, other arithmetic, per_device(): return (mixed[None], momentum_out, input_grad[None], weight_grad[None])  1.62 us
  transfers between devices with their start and end apart: 2, of which 1 were waited for; matrix products, arithmetic and copies ran while one was open for 7% of the time, Pallas kernels for 0%

profile of v1, /device:TPU:0, one launch (start us, length us, event | category | flops | bytes accessed | tf_op | source)
XLA Modules:
  0.0 77.4 jit_solution(1409896118322770474)
XLA Ops:
  8.0 0.0 copy-start
  8.0 0.0 copy-start.1
  8.0 0.0 reduce-scatter.2.cloned.1.call-start
  8.1 1.5 %copy-done = bf16[1,128,8192]{2,1,0:T(8,128)(2,1)S(1)} copy-done((bf16[1,128,8192]{2,1,0:T(8,128)(2,1)S(1)}, bf16[1,128,8192]{2,1,0:T(8,128)(2,1)}, u32[]{:S(2)}) %copy-start) | copy-done | bytes 2097176
  9.6 1.9 %convolution_convert_fusion = bf16[32,8192]{1,0:T(8,128)(2,1)} fusion(bf16[1,128,8192]{2,1,0:T(8,128)(2,1)S(1)} %copy-done, bf16[1,128,32]{1,2,0:T(8,128)(2,1)} %param.8), kind=kOutput, calls=%fused_computation | convolution fusion | flops 67371008 | bytes 2629632 | tf_op jit(solution)/shard_map/dot_general | solution.py:29
  11.5 0.0 copy-start.2
  11.5 0.0 reduce-scatter.2.cloned.1.call-update
  11.5 0.0 all-gather.4.cloned.1.call-start
  11.6 0.0 copy-done.1
  11.6 2.1 %bitcast_subtract_fusion = f32[3,8,8192]{2,1,0:T(8,128)} fusion(f32[3,8,8192]{2,1,0:T(8,128)} %param.5, f32[1,3,8,8192]{3,2,1,0:T(8,128)S(1)} %copy-done.1), kind=kLoop, calls=%fused_computation.7 | loop fusion | flops 196608 | bytes 2359296 | tf_op jit(solution)/shard_map/sub | solution.py:36
  13.7 0.0 all-gather.4.cloned.1.call-update
  13.7 0.0 copy-done.2
  13.8 12.9 %all_gather.14 = f32[3,8,8192]{2,1,0:T(8,128)} all-gather(f32[3,8,1024]{2,1,0:T(8,128)S(1)} %copy-done.2), channel_id=1, replica_groups=mesh['rep'=8,'fsdp'=4] {'rep'}, dimensions={2}, use_global_device_ids=true | all-gather | bytes 884736 | tf_op jit(solution)/shard_map/all_gather | solution.py:40
  26.7 18.1 %all-gather.1 = bf16[1,1,32,8192]{3,2,1,0:T(8,128)(2,1)S(1)} all-gather(bf16[1,1,8,8192]{3,2,1,0:T(8,128)(2,1)S(1)} %slice.7), channel_id=3, replica_groups=mesh['rep'=8,'fsdp'=4] {'fsdp'}, dimensions={2}, use_global_device_ids=true | all-gather | bytes 655360 | tf_op jit(solution)/shard_map/all_gather | solution.py:24
  44.8 1.4 %fusion.6 = bf16[1,128,32]{1,2,0:T(8,128)(2,1)} fusion(bf16[1,128,8192]{2,1,0:T(8,128)(2,1)S(1)} %copy-done, bf16[1,1,32,8192]{3,2,1,0:T(8,128)(2,1)S(1)} %all-gather.1), kind=kOutput, calls=%fused_computation.5 | convolution fusion | flops 67112960 | bytes 2629632 | tf_op jit(solution)/shard_map/dot_general | solution.py:22
  46.2 0.0 reduce-scatter.2.cloned.1.call-done
  46.2 1.6 %bitcast_convert_fusion = f32[1,8,8192]{2,1,0:T(8,128)} fusion(bf16[8,8192]{1,0:T(8,128)(2,1)} %reduce-scatter.2.cloned.1.call-done), kind=kLoop, calls=%fused_computation.13 | loop fusion | flops 65536 | bytes 393216 | tf_op jit(solution)/shard_map/broadcast_in_dim | solution.py:45
  47.8 14.7 %all-gather.4.cloned.1.call-done = f32[24,8,8192]{2,1,0:T(8,128)} async-done(((f32[3,8,8192]{2,1,0:T(8,128)}), f32[24,8,8192]{2,1,0:T(8,128)}) %all-gather.4.cloned.1.call-update) | async-done | bytes 6291472 | tf_op jit(solution)/shard_map/all_gather | solution.py:12
  62.5 4.1 %reduce_sum.9 = f32[3,8,8192]{2,1,0:T(8,128)} reduce(f32[8,3,8,8192]{3,2,1,0:T(8,128)} %bitcast.30, f32[]{:T(128)} %constant.3.clone.1), dimensions={0}, to_apply=%region_0.0 | reduce | flops 1376256 | bytes 7077892 | tf_op jit(solution)/shard_map/reduce_sum | solution.py:13
  66.6 2.7 %multiply_add_fusion = (f32[3,8,8192]{2,1,0:T(8,128)S(1)}, f32[1,3,8,8192]{3,2,1,0:T(8,128)}) fusion(f32[3,8,8192]{2,1,0:T(8,128)} %all_gather.14, f32[3,8,8192]{2,1,0:T(8,128)} %reduce_sum.9, f32[3,8,8192]{2,1,0:T(8,128)} %param.5, f32[1,3,8,8192]{3,2,1,0:T(8,128)S(1)} %copy-done.1), kind=kLoop, calls=%fused_computation.10 | loop fusion | flops 1769472 | bytes 4718592 | tf_op jit(solution)/shard_map/add | solution.py:41
  69.3 0.6 constant_dynamic-slice_fusion
  (1 shorter events, 0.0 us)
Async XLA Ops:
  8.0 1.6 %copy-start = (bf16[1,128,8192]{2,1,0:T(8,128)(2,1)S(1)}, bf16[1,128,8192]{2,1,0:T(8,128)(2,1)}, u32[]{:S(2)}) copy-start(bf16[1,128,8192]{2,1,0:T(8,128)(2,1)} %param.9) | copy-start | bytes 6291460
  8.0 3.6 %copy-start.1 = (f32[1,3,8,8192]{3,2,1,0:T(8,128)S(1)}, f32[1,3,8,8192]{3,2,1,0:T(8,128)}, u32[]{:S(2)}) copy-start(f32[1,3,8,8192]{3,2,1,0:T(8,128)} %param.6) | copy-start | bytes 2359300
  8.0 38.2 %reduce-scatter.2.cloned.1.call-start = ((), (), s32[]{:S(2)}) async-start(), calls=%async_computation.1 | async-start | bytes 655360 | tf_op jit(solution)/shard_map/reduce_scatter | solution.py:28
  11.5 2.2 %copy-start.2 = (f32[3,8,1024]{2,1,0:T(8,128)S(1)}, f32[3,8,1024]{2,1,0:T(8,128)}, u32[]{:S(2)}) copy-start(f32[3,8,1024]{2,1,0:T(8,128)} %param.7) | copy-start | bytes 294916
  11.5 51.0 %all-gather.4.cloned.1.call-start = ((), (), s32[]{:S(2)}) async-start(), calls=%async_computation.2 | async-start | bytes 7077888 | tf_op jit(solution)/shard_map/all_gather | solution.py:12
Sparse Core Ops, SparseCore 0:
  11.7 26.2 reduce-scatter.1
Sparse Core Ops, SparseCore 1:
  14.5 48.0 all-gather.3
